TPU v7x, 32 devices: a whole 2x2x4 slice. The times are simulated.
32 devices in a mesh: groups: 2 (over x), head: 8 (over z, y), tensor: 2 (over core).
Axes of the slice: x: 2, y: 2, z: 4, core: 2. Of those that a mesh axis runs over, the one named last changes fastest.
Arguments:
- query: bfloat16 [8192, 1024], P(('groups', 'head'), 'tensor'), parts along dimension 0, may hold values from -32 to 32
- keys_in: bfloat16 [8192, 1024], P(('groups', 'head'), 'tensor'), parts along dimension 0, may hold values from -6 to 6
- values_in: bfloat16 [8192, 1024], P(('groups', 'head'), 'tensor'), parts along dimension 0, may hold values from -6 to 6
- grad_out: bfloat16 [8192, 1024], P(('groups', 'head'), 'tensor'), parts along dimension 0, may hold values from -96 to 96
- w_out: bfloat16 [1024, 1024], P('tensor'), may hold values from -0.1875 to 0.1875
- w_query: bfloat16 [1024, 1024], P(None, 'tensor'), may hold values from -0.1875 to 0.1875
- w_key: bfloat16 [1024, 1024], P(None, 'tensor'), may hold values from -0.1875 to 0.1875
- w_value: bfloat16 [1024, 1024], P(None, 'tensor'), may hold values from -0.1875 to 0.1875
- perm: int32 [2, 4096], P('groups'), parts along dimension 0, may hold values from 0 to 4095, as said below
- blocks: int32 [2, 32, 12], P('groups'), parts along dimension 0, may hold values from 0 to 31, as said below
- counts: int32 [2, 32], P('groups'), parts along dimension 0, may hold values from 1 to 12
Outputs:
- input_grad: bfloat16 [8192, 1024], P(('groups', 'head', 'tensor')), parts along dimension 0
There are 2 independent parts, one for each index of `groups`. A program takes and returns all parts, laid end to end along the dimension named above; an argument that names none is the same for every part. Nothing has to cross between parts.
Inputs may be any that keep to these rules, and one draw needn't show every extreme that they name: Each row of perm holds every node number of the graph once. blocks[g, b, 0] is b; the 12 entries of blocks[g, b] are different block numbers.
All inputs are finite; a program needn't handle non-finite values.
Results may differ from a plain program's by a relative error of at most 0.011.
Values may be sent and summed in bfloat16 or wider, within the bound.
A program may use at most 64 MiB of HBM per device.

v0:
```python
import jax
import jax.numpy as jnp
from jax import lax
from jax.sharding import PartitionSpec as P

HD = 64
BS = 128
KB = 12


def on_device(
    query, keys_in, values_in, grad_out, w_out, w_query, w_key, w_value, perm, blocks, counts
):
    local_rows, half_width = query.shape
    graph_count, graph_nodes = perm.shape
    half_heads = half_width // HD
    part_rows = local_rows // graph_count
    block_count = graph_nodes // BS
    group_size = 512 // BS
    scale = HD ** (-0.5)
    attn_grad = lax.dot_general(
        lax.all_gather(grad_out, "tensor", axis=1, tiled=True),
        w_out,
        (((1,), (1,)), ((), ())),
        preferred_element_type=jnp.float32,
    ).astype(jnp.bfloat16)
    shaped = [
        member.reshape(part_rows, graph_count * half_heads, HD)
        for member in (query, keys_in, values_in, attn_grad)
    ]
    packed = jnp.stack(shaped, axis=2).reshape(part_rows, graph_count * half_heads, 4 * HD)
    arrived = lax.all_to_all(packed, "head", split_axis=1, concat_axis=0, tiled=True).reshape(
        graph_nodes, 4, HD
    )
    position = lax.axis_index("head")
    graph = position // half_heads
    order = lax.dynamic_index_in_dim(perm, graph, 0, keepdims=False)
    inverse = (
        jnp.zeros((graph_nodes,), jnp.int32).at[order].set(jnp.arange(graph_nodes, dtype=jnp.int32))
    )
    by_node = jnp.take(arrived, inverse, axis=0).reshape(block_count, BS, 4, HD)
    query_blk = by_node[:, :, 0]
    keyval = by_node[:, :, 1:3].reshape(block_count, BS, 2 * HD)
    grad_blk = by_node[:, :, 3]
    block_row = lax.dynamic_index_in_dim(blocks, graph, 0, keepdims=False)
    count_row = lax.dynamic_index_in_dim(counts, graph, 0, keepdims=False)
    live = jnp.arange(KB, dtype=jnp.int32)[None, :] < count_row[:, None]

    def one_group(carry, first):
        queries = lax.dynamic_slice_in_dim(query_blk, first, group_size, 0)
        grads = lax.dynamic_slice_in_dim(grad_blk, first, group_size, 0)
        listed = lax.dynamic_slice_in_dim(block_row, first, group_size, 0)
        active = lax.dynamic_slice_in_dim(live, first, group_size, 0)
        fetched = jnp.take(keyval, listed, axis=0)
        fetched_keys = fetched[..., :HD]
        fetched_values = fetched[..., HD:]
        score = (
            jnp.einsum("qad,qjcd->qajc", queries, fetched_keys, preferred_element_type=jnp.float32)
            * scale
        )
        score = jnp.where(active[:, None, :, None], score, -jnp.inf)
        top = jnp.max(score, axis=(2, 3), keepdims=True)
        expo = jnp.exp(score - top)
        prob = expo / jnp.sum(expo, axis=(2, 3), keepdims=True)
        prob_b = prob.astype(jnp.bfloat16)
        attn = jnp.einsum(
            "qajc,qjcd->qad", prob_b, fetched_values, preferred_element_type=jnp.float32
        )
        delta = jnp.sum(grads.astype(jnp.float32) * attn, axis=-1)
        dprob = jnp.einsum(
            "qad,qjcd->qajc", grads, fetched_values, preferred_element_type=jnp.float32
        )
        dscore = (prob * (dprob - delta[:, :, None, None])).astype(jnp.bfloat16)
        query_grad = (
            jnp.einsum("qajc,qjcd->qad", dscore, fetched_keys, preferred_element_type=jnp.float32)
            * scale
        )
        key_terms = (
            jnp.einsum("qajc,qad->qjcd", dscore, queries, preferred_element_type=jnp.float32)
            * scale
        )
        value_terms = jnp.einsum(
            "qajc,qad->qjcd", prob_b, grads, preferred_element_type=jnp.float32
        )
        update = jnp.concatenate((key_terms, value_terms), axis=-1)
        return (carry.at[listed].add(update), query_grad)

    firsts = jnp.arange(block_count // group_size, dtype=jnp.int32) * group_size
    keyval_grad, query_grads = lax.scan(
        one_group, jnp.zeros((block_count, BS, 2 * HD), jnp.float32), firsts
    )
    all_grads = jnp.concatenate(
        (query_grads.reshape(graph_nodes, HD), keyval_grad.reshape(graph_nodes, 2 * HD)), axis=1
    )
    all_grads = all_grads.astype(jnp.bfloat16)
    by_part = jnp.take(all_grads, order, axis=0).reshape(graph_nodes, 1, 3 * HD)
    returned = lax.all_to_all(by_part, "head", split_axis=0, concat_axis=1, tiled=True).reshape(
        local_rows, half_heads, 3, HD
    )
    full_width = w_query.shape[0]

    def term_for(weight, member):
        shaped_weight = weight.reshape(full_width, half_heads, HD)
        piece = returned[:, :, member]
        return jnp.einsum("rhd,ehd->re", piece, shaped_weight, preferred_element_type=jnp.float32)

    total = lax.psum_scatter(term_for(w_query, 0), "tensor", scatter_dimension=0, tiled=True)
    total = total + lax.psum_scatter(term_for(w_key, 1), "tensor", scatter_dimension=0, tiled=True)
    total = total + lax.psum_scatter(
        term_for(w_value, 2), "tensor", scatter_dimension=0, tiled=True
    )
    return total.astype(jnp.bfloat16)


def solution(mesh):
    return jax.shard_map(
        on_device,
        mesh=mesh,
        in_specs=(
            P(("groups", "head"), "tensor"),
            P(("groups", "head"), "tensor"),
            P(("groups", "head"), "tensor"),
            P(("groups", "head"), "tensor"),
            P("tensor", None),
            P(None, "tensor"),
            P(None, "tensor"),
            P(None, "tensor"),
            P("groups", None),
            P("groups", None, None),
            P("groups", None),
        ),
        out_specs=P(("groups", "head", "tensor"), None),
        check_vma=False,
    )
```

profile of v0, /device:TPU:0, one launch (start us, length us, event | category | flops | bytes accessed | tf_op | source)
XLA Modules:
  0.0 487.7 jit_solution(12786083107851520610)
XLA Ops:
  10.0 10.7 %all-gather.2.cloned.1.call-done = bf16[512,1024]{1,0:T(8,128)(2,1)} async-done(((bf16[512,512]{1,0:T(8,128)(2,1)}), bf16[512,1024]{1,0:T(8,128)(2,1)}) %all-gather.2.cloned.1.call-update) | async-done | bytes 1048592 | tf_op jit(solution)/shard_map/all_gather | solution.py:22
  24.5 5.9 %all-to-all-start = ((bf16[512,8,256]{0,2,1:T(8,128)(2,1)}), bf16[512,8,256]{0,2,1:T(8,128)(2,1)S(1)}, u32[]{:S(2)}, u32[]{:S(2)}) async-start(bf16[512,8,256]{0,2,1:T(8,128)(2,1)} %bitcast.136), calls=%async_computation | async-start | bytes 4194304 | tf_op jit(solution)/shard_map/all_to_all | solution.py:32
  30.5 15.7 %scatter_custom_fusion.1 = s32[4096]{0:T(1024)S(1)} fusion(s32[4096]{0:T(1024)S(1)} %bitcast.150, s32[4096]{0:T(1024)S(1)} %iota.11, s32[]{:T(128)} %constant.74.clone.1), kind=kCustom, calls=%fused_computation.62 | custom fusion | bytes 16388 | tf_op jit(solution)/shard_map/scatter | solution.py:39
  46.4 32.7 %all-to-all-done = bf16[512,8,256]{0,2,1:T(8,128)(2,1)S(1)} async-done(((bf16[512,8,256]{0,2,1:T(8,128)(2,1)}), bf16[512,8,256]{0,2,1:T(8,128)(2,1)S(1)}, u32[]{:S(2)}, u32[]{:S(2)}) %all-to-all-start) | async-done | bytes 2097184 | tf_op jit(solution)/shard_map/all_to_all | solution.py:32
  80.4 2.8 copy.144
  83.3 3.3 reshape.170
  86.5 30.7 %gather_fusion.1 = bf16[4096,4,64]{2,1,0:T(4,128)(2,1)} fusion(bf16[4096,4,64]{2,1,0:T(4,128)(2,1)} %reshape.170, s32[4096]{0:T(1024)S(1)} %fusion.24), kind=kCustom, calls=%fused_computation.1 | custom fusion | bytes 4210688 | tf_op jit(solution)/shard_map/jit(_take)/gather | solution.py:41
  117.2 4.8 copy.145
  125.9 248.2 %while.12 = (s32[]{:T(128)}, f32[32,128,128]{2,1,0:T(8,128)}, bf16[8,4,128,64]{2,3,1,0:T(8,128)(2,1)}, s32[8]{0:T(128)S(1)}, s32[32,12]{1,0:T(8,128)S(1)}, /*ind...) while((s32[]{:T(128)}, f32[32,128,128]{2,1,0:T(8,128)}, ...), condition=%wide.region_6.7_spmd, body=%wide.region_1.0_spmd.sunk | while | flops 625737472 | bytes 73627488 | solution.py:89
  134.9 2.7 multiply_convert_fusion.2
  137.7 2.1 convolution_multiply_fusion.2
  140.7 2.0 pad_maximum_fusion.4
  142.7 2.4 copy.192
  145.1 9.1 %scatter_fusion = f32[32,128,128]{2,1,0:T(8,128)} fusion(f32[32,128,128]{2,1,0:T(8,128)} %get-tuple-element.203, s32[48]{0:T(128)S(1)} %reshape.184, f32[48,128,128]{2,1,0:T(8,128)S(1)} %copy.192), kind=kCustom, calls=%fused_computation.3.clone.1 | custom fusion | flops 786432 | bytes 9437376 | tf_op jit(solution)/shard_map/while/body/eval_jaxpr/scatter-add | solution.py:86
  154.2 2.8 fusion.62
  166.0 2.7 multiply_convert_fusion.2
  168.8 2.1 convolution_multiply_fusion.2
  173.8 2.4 copy.192
  176.2 9.0 %scatter_fusion = f32[32,128,128]{2,1,0:T(8,128)} fusion(f32[32,128,128]{2,1,0:T(8,128)} %get-tuple-element.203, s32[48]{0:T(128)S(1)} %reshape.184, f32[48,128,128]{2,1,0:T(8,128)S(1)} %copy.192), kind=kCustom, calls=%fused_computation.3.clone.1 | custom fusion | flops 786432 | bytes 9437376 | tf_op jit(solution)/shard_map/while/body/eval_jaxpr/scatter-add | solution.py:86
  185.3 2.8 fusion.62
  197.1 2.7 multiply_convert_fusion.2
  199.9 2.1 convolution_multiply_fusion.2
  204.9 2.4 copy.192
  207.3 9.0 %scatter_fusion = f32[32,128,128]{2,1,0:T(8,128)} fusion(f32[32,128,128]{2,1,0:T(8,128)} %get-tuple-element.203, s32[48]{0:T(128)S(1)} %reshape.184, f32[48,128,128]{2,1,0:T(8,128)S(1)} %copy.192), kind=kCustom, calls=%fused_computation.3.clone.1 | custom fusion | flops 786432 | bytes 9437376 | tf_op jit(solution)/shard_map/while/body/eval_jaxpr/scatter-add | solution.py:86
  216.3 2.8 fusion.62
  228.1 2.7 multiply_convert_fusion.2
  230.9 2.1 convolution_multiply_fusion.2
  235.9 2.4 copy.192
  238.3 9.0 %scatter_fusion = f32[32,128,128]{2,1,0:T(8,128)} fusion(f32[32,128,128]{2,1,0:T(8,128)} %get-tuple-element.203, s32[48]{0:T(128)S(1)} %reshape.184, f32[48,128,128]{2,1,0:T(8,128)S(1)} %copy.192), kind=kCustom, calls=%fused_computation.3.clone.1 | custom fusion | flops 786432 | bytes 9437376 | tf_op jit(solution)/shard_map/while/body/eval_jaxpr/scatter-add | solution.py:86
  247.3 2.8 fusion.62
  259.1 2.7 multiply_convert_fusion.2
  261.9 2.1 convolution_multiply_fusion.2
  264.9 2.0 pad_maximum_fusion.4
  266.9 2.4 copy.192
  269.3 9.0 %scatter_fusion = f32[32,128,128]{2,1,0:T(8,128)} fusion(f32[32,128,128]{2,1,0:T(8,128)} %get-tuple-element.203, s32[48]{0:T(128)S(1)} %reshape.184, f32[48,128,128]{2,1,0:T(8,128)S(1)} %copy.192), kind=kCustom, calls=%fused_computation.3.clone.1 | custom fusion | flops 786432 | bytes 9437376 | tf_op jit(solution)/shard_map/while/body/eval_jaxpr/scatter-add | solution.py:86
  278.3 2.8 fusion.62
  290.1 2.7 multiply_convert_fusion.2
  292.9 2.1 convolution_multiply_fusion.2
  296.0 2.0 pad_maximum_fusion.4
  298.0 2.4 copy.192
  300.3 9.0 %scatter_fusion = f32[32,128,128]{2,1,0:T(8,128)} fusion(f32[32,128,128]{2,1,0:T(8,128)} %get-tuple-element.203, s32[48]{0:T(128)S(1)} %reshape.184, f32[48,128,128]{2,1,0:T(8,128)S(1)} %copy.192), kind=kCustom, calls=%fused_computation.3.clone.1 | custom fusion | flops 786432 | bytes 9437376 | tf_op jit(solution)/shard_map/while/body/eval_jaxpr/scatter-add | solution.py:86
  309.4 2.8 fusion.62
  321.1 2.7 multiply_convert_fusion.2
  323.9 2.1 convolution_multiply_fusion.2
  328.9 2.4 copy.192
  331.3 9.0 %scatter_fusion = f32[32,128,128]{2,1,0:T(8,128)} fusion(f32[32,128,128]{2,1,0:T(8,128)} %get-tuple-element.203, s32[48]{0:T(128)S(1)} %reshape.184, f32[48,128,128]{2,1,0:T(8,128)S(1)} %copy.192), kind=kCustom, calls=%fused_computation.3.clone.1 | custom fusion | flops 786432 | bytes 9437376 | tf_op jit(solution)/shard_map/while/body/eval_jaxpr/scatter-add | solution.py:86
  340.3 2.8 fusion.62
  352.1 2.7 multiply_convert_fusion.2
  354.8 2.1 convolution_multiply_fusion.2
  357.9 2.0 pad_maximum_fusion.4
  359.9 2.4 copy.192
  362.3 9.0 %scatter_fusion = f32[32,128,128]{2,1,0:T(8,128)} fusion(f32[32,128,128]{2,1,0:T(8,128)} %get-tuple-element.203, s32[48]{0:T(128)S(1)} %reshape.184, f32[48,128,128]{2,1,0:T(8,128)S(1)} %copy.192), kind=kCustom, calls=%fused_computation.3.clone.1 | custom fusion | flops 786432 | bytes 9437376 | tf_op jit(solution)/shard_map/while/body/eval_jaxpr/scatter-add | solution.py:86
  371.3 2.8 fusion.62
  378.3 16.9 %gather_fusion.2 = bf16[4096,192]{1,0:T(8,128)(2,1)} fusion(bf16[4096,192]{1,0:T(8,128)(2,1)S(1)} %pad_maximum_fusion.2, s32[4096]{0:T(1024)S(1)} %broadcast_clamp_fusion), kind=kCustom, calls=%fused_computation.2 | custom fusion | bytes 3162112 | tf_op jit(solution)/shard_map/jit(_take)/gather | solution.py:96
  397.7 3.1 reduce
  400.8 6.7 %reshape.173 = bf16[8,2,49152]{2,1,0:T(2,128)(2,1)} reshape(bf16[4096,192]{1,0:T(8,128)(2,1)} %reduce) | data formatting | bytes 3145728
  407.5 3.8 all-to-all-start.1
  412.6 2.4 copy.132
  416.3 32.2 %all-to-all-done.1 = bf16[8,2,49152]{2,1,0:T(2,128)(2,1)S(1)} async-done(((bf16[8,2,49152]{2,1,0:T(2,128)(2,1)}), bf16[8,2,49152]{2,1,0:T(2,128)(2,1)S(1)}, u32[]{:S(2)}, u32[]{:S(2)}) %all-to-all-start.1) | async-done | bytes 1572896 | tf_op jit(solution)/shard_map/all_to_all | solution.py:97
  448.4 4.9 %reshape.174 = bf16[4096,1,192]{2,1,0:T(2,128)(2,1)} reshape(bf16[8,2,49152]{2,1,0:T(2,128)(2,1)S(1)} %all-to-all-done.1) | data formatting | bytes 3145728
  453.3 9.9 %copy.127 = bf16[4096,1,192]{0,2,1:T(8,128)(2,1)S(1)} copy(bf16[4096,1,192]{2,1,0:T(2,128)(2,1)} %reshape.174) | data formatting | bytes 3145728 | tf_op jit(solution)/shard_map/all_to_all | solution.py:97
  467.6 2.1 bitcast_add_fusion
  469.7 9.0 %reduce-scatter.2.cloned.1.call-done = f32[256,1024]{1,0:T(8,128)} async-done(((f32[512,1024]{1,0:T(8,128)}), f32[256,1024]{1,0:T(8,128)}) %reduce-scatter.2.cloned.1.call-update) | async-done | bytes 1048592 | tf_op jit(solution)/shard_map/reduce_scatter | solution.py:107
  478.7 2.1 convert_element_type.17
  (208 shorter events, 99.0 us)
Async XLA Ops:
  6.5 14.1 %copy-start = (bf16[512,1024]{1,0:T(8,128)(2,1)S(1)}, bf16[512,1024]{1,0:T(8,128)(2,1)}, u32[]{:S(2)}) copy-start(bf16[512,1024]{1,0:T(8,128)(2,1)} %param.17) | copy-start | bytes 3145732
  6.5 3.2 copy-start.11
  6.5 14.1 %all-gather.2.cloned.1.call-start = ((), (), s32[]{:S(2)}) async-start(), calls=%async_computation.3 | async-start | bytes 1572864 | tf_op jit(solution)/shard_map/all_gather | solution.py:22
  24.5 5.9 %copy-start.13 = (s32[1,32,12]{1,0,2:T(1,128)S(1)}, s32[1,32,12]{1,0,2:T(1,128)}, u32[]{:S(2)}) copy-start(s32[1,32,12]{1,0,2:T(1,128)} %param.22) | copy-start | bytes 4612
  24.5 6.0 %copy-start.12 = (s32[1,4096]{1,0:T(1,128)S(1)}, s32[1,4096]{1,0:T(1,128)}, u32[]{:S(2)}) copy-start(s32[1,4096]{1,0:T(1,128)} %param.21) | copy-start | bytes 49156
  24.5 21.8 %copy-start.14 = (s32[1,32]{1,0:T(1,128)S(1)}, s32[1,32]{1,0:T(1,128)}, u32[]{:S(2)}) copy-start(s32[1,32]{1,0:T(1,128)} %param.23) | copy-start | bytes 388
  24.5 54.6 %all-to-all-start = ((bf16[512,8,256]{0,2,1:T(8,128)(2,1)}), bf16[512,8,256]{0,2,1:T(8,128)(2,1)S(1)}, u32[]{:S(2)}, u32[]{:S(2)}) async-start(bf16[512,8,256]{0,2,1:T(8,128)(2,1)} %bitcast.136), calls=%async_computation | async-start | bytes 4194304 | tf_op jit(solution)/shard_map/all_to_all | solution.py:32
  79.1 1.3 copy-start.5
  125.9 2.7 copy-start.3
  130.6 4.3 copy-start.2
  154.2 2.8 copy-start.4
  157.0 2.7 copy-start.3
  161.7 4.3 copy-start.2
  185.3 2.8 copy-start.4
  188.1 2.7 copy-start.3
  192.8 4.3 copy-start.2
  216.3 2.8 copy-start.4
  219.1 2.7 copy-start.3
  223.8 4.3 copy-start.2
  247.3 2.8 copy-start.4
  250.1 2.7 copy-start.3
  254.8 4.3 copy-start.2
  278.3 2.8 copy-start.4
  281.1 2.7 copy-start.3
  285.8 4.3 copy-start.2
  309.4 2.8 copy-start.4
  312.2 2.7 copy-start.3
  316.9 4.2 copy-start.2
  340.3 2.8 copy-start.4
  343.1 2.7 copy-start.3
  347.9 4.2 copy-start.2
  371.3 2.8 copy-start.4
  407.5 3.8 copy-start.6
  407.5 41.0 %all-to-all-start.1 = ((bf16[8,2,49152]{2,1,0:T(2,128)(2,1)}), bf16[8,2,49152]{2,1,0:T(2,128)(2,1)S(1)}, u32[]{:S(2)}, u32[]{:S(2)}) async-start(bf16[8,2,49152]{2,1,0:T(2,128)(2,1)} %reshape.173), calls=%async_computation.1 | async-start | bytes 3145728 | tf_op jit(solution)/shard_map/all_to_all | solution.py:97
  411.3 67.5 %reduce-scatter.2.cloned.1.call-start = ((), (), s32[]{:S(2)}) async-start(), calls=%async_computation.4 | async-start | bytes 3145728 | tf_op jit(solution)/shard_map/reduce_scatter | solution.py:107
  412.6 2.4 copy-start.7
  463.9 1.2 copy-start.10
  465.1 1.2 copy-start.9
  466.3 1.2 copy-start.8
  467.6 13.3 %copy-start.1 = (bf16[512,1024]{1,0:T(8,128)(2,1)S(1)}, bf16[512,1024]{1,0:T(8,128)(2,1)}, u32[]{:S(2)}) copy-start(bf16[512,1024]{1,0:T(8,128)(2,1)} %param.17) | copy-start | bytes 3145732
Sparse Core Ops, SparseCore 0:
  8.9 11.7 all-gather.1
  469.8 8.8 reduce-scatter.1
where the time goes:
time: 491 us; the launch traced here: 488 us
  local copies, waits for them, and re-layouts  166 us (34%)
  other arithmetic  107 us (22%)
  matrix products  90.5 us (18%)
  waiting for transfers between devices  85.3 us (17%)
  loops' own time  15.5 us (3%)
  between operations  13.6 us (3%)
  starting transfers between devices  9.72 us (2%)
    scatter-add x8, other arithmetic, one_group(): return (carry.at[listed].add(update), query_grad)  72.1 us
    gather x2, local copies, waits for them, and re-layouts, on_device(): by_node = jnp.take(arrived, inverse, axis=0).reshape(block_count, BS, 4, HD)  35.5 us
    all_to_all x1, waiting for transfers between devices, on_device(): lax.all_to_all(packed, 'head', split_axis=1, concat_axis=0, tiled=True)  32.7 us
    all_to_all x1, waiting for transfers between devices, on_device(): lax.all_to_all(by_part, 'head', split_axis=0, concat_axis=1, tiled=True)  32.2 us
    unnamed x34, local copies, waits for them, and re-layouts  23.4 us
    dot_general x8, matrix products, one_group(): jnp.einsum('qajc,qjcd->qad', dscore, fetched_keys, preferred_element_type...  22.4 us
    dot_general x8, matrix products, one_group(): jnp.einsum('qad,qjcd->qajc', grads, fetched_values, preferred_element_typ...  22 us
    concatenate x8, local copies, waits for them, and re-layouts, one_group(): update = jnp.concatenate((key_terms, value_terms), axis=-1)  19 us
  transfers between devices with their start and end apart: 4, of which 4 were waited for; matrix products, arithmetic and copies ran while one was open for 5% of the time, Pallas kernels for 0%

commit v1 on v0

--- a/solution.py
+++ b/solution.py
@@ -2,6 +2,7 @@
 import jax.numpy as jnp
 from jax import lax
 from jax.sharding import PartitionSpec as P
+from jax.lax import axis_index, axis_size, ppermute
 
 HD = 64
 BS = 128
@@ -94,9 +95,26 @@
     )
     all_grads = all_grads.astype(jnp.bfloat16)
     by_part = jnp.take(all_grads, order, axis=0).reshape(graph_nodes, 1, 3 * HD)
-    returned = lax.all_to_all(by_part, "head", split_axis=0, concat_axis=1, tiled=True).reshape(
-        local_rows, half_heads, 3, HD
-    )
+
+    def drive_the_node(row_data):
+        met_up = axis_size("head")
+        far_arr, s_next = (met_up, axis_index("head"))
+        after = row_data.shape[0] // far_arr
+        val = list(row_data.shape)
+        val[0] = after
+        e_next = val[1]
+        val[1] = e_next * far_arr
+        later = jnp.zeros(val, row_data.dtype)
+        for idx in range(far_arr):
+            extra = lax.dynamic_slice_in_dim(row_data, (s_next ^ idx) * after, after, axis=0)
+            if idx:
+                extra = ppermute(
+                    extra, "head", perm=list(map(lambda d: (d, d ^ idx), range(far_arr)))
+                )
+            later = lax.dynamic_update_slice_in_dim(later, extra, (s_next ^ idx) * e_next, axis=1)
+        return later
+
+    returned = drive_the_node(by_part).reshape(local_rows, half_heads, 3, HD)
     full_width = w_query.shape[0]
 
     def term_for(weight, member):

time: 491 us -> 468 us (0.953)
  local copies, waits for them, and re-layouts: 166 us -> 149 us
  waiting for transfers between devices: 85.3 us -> 73.3 us
  starting transfers between devices: 9.72 us -> 16 us
    all_to_all x1 -> x0, waiting for transfers between devices: 32.2 us -> none  [on_device(): lax.all_to_all(by_part, 'head', split_axis=0, concat_axis=1, tiled=True)]
    ppermute x0 -> x7, waiting for transfers between devices: none -> 19.9 us  [drive_the_node(): ppermute(extra, 'head', perm=list(map(lambda d: (d, d ^ idx), range(far_a...]
    unnamed x34 -> x29, local copies, waits for them, and re-layouts: 23.4 us -> 9.69 us
    ppermute x0 -> x7, starting transfers between devices: none -> 10 us  [drive_the_node(): ppermute(extra, 'head', perm=list(map(lambda d: (d, d ^ idx), range(far_a...]
    all_to_all x1 -> x0, local copies, waits for them, and re-layouts: 9.89 us -> none  [on_device(): lax.all_to_all(by_part, 'head', split_axis=0, concat_axis=1, tiled=True)]
    reduce_scatter x1, waiting for transfers between devices: 9.05 us -> 14.5 us  [on_device(): lax.psum_scatter(term_for(w_query, 0), 'tensor', scatter_dimension=0, til...]
    all_to_all x1, waiting for transfers between devices: 32.7 us -> 27.5 us  [on_device(): lax.all_to_all(packed, 'head', split_axis=1, concat_axis=0, tiled=True)]
  transfers between devices with their start and end apart: 4 -> 10, of which waited for: 4 -> 7; matrix products, arithmetic and copies ran while one was open for 5% -> 6% of each run, Pallas kernels for 0% -> 0%
where the time goes in v1:
time: 468 us; the launch traced here: 464 us
  local copies, waits for them, and re-layouts  149 us (32%)
  other arithmetic  104 us (22%)
  matrix products  91.4 us (20%)
  waiting for transfers between devices  73.3 us (16%)
  loops' own time  17.1 us (4%)
  starting transfers between devices  16 us (3%)
  between operations  13.9 us (3%)
    scatter-add x8, other arithmetic, one_group(): return (carry.at[listed].add(update), query_grad)  72.6 us
    gather x2, local copies, waits for them, and re-layouts, on_device(): by_node = jnp.take(arrived, inverse, axis=0).reshape(block_count, BS, 4, HD)  35.7 us
    all_to_all x1, waiting for transfers between devices, on_device(): lax.all_to_all(packed, 'head', split_axis=1, concat_axis=0, tiled=True)  27.5 us
    dot_general x8, matrix products, one_group(): jnp.einsum('qajc,qjcd->qad', dscore, fetched_keys, preferred_element_type...  22.4 us
    dot_general x8, matrix products, one_group(): jnp.einsum('qad,qjcd->qajc', grads, fetched_values, preferred_element_typ...  21.6 us
    ppermute x7, waiting for transfers between devices, drive_the_node(): ppermute(extra, 'head', perm=list(map(lambda d: (d, d ^ idx), range(far_a...  19.9 us
    concatenate x8, local copies, waits for them, and re-layouts, one_group(): update = jnp.concatenate((key_terms, value_terms), axis=-1)  19 us
    another operation x1, loops' own time, on_device(): lax.scan(one_group, jnp.zeros((block_count, BS, 2 * HD), jnp.float32), fi...  17.1 us
  transfers between devices with their start and end apart: 10, of which 7 were waited for; matrix products, arithmetic and copies ran while one was open for 6% of the time, Pallas kernels for 0%

profile of v1, /device:TPU:0, one launch (start us, length us, event | category | flops | bytes accessed | tf_op | source)
XLA Modules:
  0.0 464.4 jit_solution(14963507805512819056)
XLA Ops:
  10.0 10.7 %all-gather.2.cloned.1.call-done = bf16[512,1024]{1,0:T(8,128)(2,1)} async-done(((bf16[512,512]{1,0:T(8,128)(2,1)}), bf16[512,1024]{1,0:T(8,128)(2,1)}) %all-gather.2.cloned.1.call-update) | async-done | bytes 1048592 | tf_op jit(solution)/shard_map/all_gather | solution.py:23
  24.5 5.9 %all-to-all-start = ((bf16[512,8,256]{0,2,1:T(8,128)(2,1)}), bf16[512,8,256]{0,2,1:T(8,128)(2,1)S(1)}, u32[]{:S(2)}, u32[]{:S(2)}) async-start(bf16[512,8,256]{0,2,1:T(8,128)(2,1)} %bitcast.137), calls=%async_computation | async-start | bytes 4194304 | tf_op jit(solution)/shard_map/all_to_all | solution.py:33
  32.0 2.4 copy.82
  35.7 15.7 %scatter_custom_fusion.1 = s32[4096]{0:T(1024)S(1)} fusion(s32[4096]{0:T(1024)S(1)} %bitcast.158, s32[4096]{0:T(1024)S(1)} %iota.11, s32[]{:T(128)} %constant.57.clone.1), kind=kCustom, calls=%fused_computation.63 | custom fusion | bytes 16388 | tf_op jit(solution)/shard_map/scatter | solution.py:40
  51.6 27.5 %all-to-all-done = bf16[512,8,256]{0,2,1:T(8,128)(2,1)S(1)} async-done(((bf16[512,8,256]{0,2,1:T(8,128)(2,1)}), bf16[512,8,256]{0,2,1:T(8,128)(2,1)S(1)}, u32[]{:S(2)}, u32[]{:S(2)}) %all-to-all-start) | async-done | bytes 2097184 | tf_op jit(solution)/shard_map/all_to_all | solution.py:33
  80.4 2.8 copy.94
  83.3 3.2 reshape.154
  86.5 30.9 %gather_fusion.1 = bf16[4096,4,64]{2,1,0:T(4,128)(2,1)} fusion(bf16[4096,4,64]{2,1,0:T(4,128)(2,1)} %reshape.154, s32[4096]{0:T(1024)S(1)} %fusion.24), kind=kCustom, calls=%fused_computation.1 | custom fusion | bytes 4210688 | tf_op jit(solution)/shard_map/jit(_take)/gather | solution.py:42
  117.4 4.8 %copy.95 = bf16[32,128,4,64]{1,0,3,2:T(8,128)(2,1)S(1)} copy(bf16[32,128,4,64]{3,2,1,0:T(4,128)(2,1)} %bitcast.135) | data formatting | bytes 4194304 | tf_op jit(solution)/shard_map/jit(_take)/gather | solution.py:42
  126.2 250.3 %while.12 = (s32[]{:T(128)}, f32[32,128,128]{2,1,0:T(8,128)}, bf16[8,4,128,64]{2,3,1,0:T(8,128)(2,1)}, s32[8]{0:T(128)S(1)}, s32[32,12]{1,0:T(8,128)S(1)}, /*ind...) while((s32[]{:T(128)}, f32[32,128,128]{2,1,0:T(8,128)}, ...), condition=%wide.region_6.7_spmd, body=%wide.region_1.0_spmd.sunk | while | flops 625737472 | bytes 73627488 | solution.py:90
  135.5 2.7 multiply_convert_fusion.2
  138.2 2.1 convolution_multiply_fusion.2
  141.2 2.0 pad_maximum_fusion.4
  143.2 2.4 copy.131
  145.6 9.1 %scatter_fusion = f32[32,128,128]{2,1,0:T(8,128)} fusion(f32[32,128,128]{2,1,0:T(8,128)} %get-tuple-element.190, s32[48]{0:T(128)S(1)} %reshape.166, f32[48,128,128]{2,1,0:T(8,128)S(1)} %copy.131), kind=kCustom, calls=%fused_computation.3.clone.1 | custom fusion | flops 786432 | bytes 9437376 | tf_op jit(solution)/shard_map/while/body/eval_jaxpr/scatter-add | solution.py:87
  154.7 2.8 fusion.61
  166.8 2.7 multiply_convert_fusion.2
  169.5 2.1 convolution_multiply_fusion.2
  174.5 2.4 copy.131
  176.9 9.1 %scatter_fusion = f32[32,128,128]{2,1,0:T(8,128)} fusion(f32[32,128,128]{2,1,0:T(8,128)} %get-tuple-element.190, s32[48]{0:T(128)S(1)} %reshape.166, f32[48,128,128]{2,1,0:T(8,128)S(1)} %copy.131), kind=kCustom, calls=%fused_computation.3.clone.1 | custom fusion | flops 786432 | bytes 9437376 | tf_op jit(solution)/shard_map/while/body/eval_jaxpr/scatter-add | solution.py:87
  186.0 2.8 fusion.61
  198.1 2.7 multiply_convert_fusion.2
  200.8 2.1 convolution_multiply_fusion.2
  205.9 2.4 copy.131
  208.3 9.1 %scatter_fusion = f32[32,128,128]{2,1,0:T(8,128)} fusion(f32[32,128,128]{2,1,0:T(8,128)} %get-tuple-element.190, s32[48]{0:T(128)S(1)} %reshape.166, f32[48,128,128]{2,1,0:T(8,128)S(1)} %copy.131), kind=kCustom, calls=%fused_computation.3.clone.1 | custom fusion | flops 786432 | bytes 9437376 | tf_op jit(solution)/shard_map/while/body/eval_jaxpr/scatter-add | solution.py:87
  217.4 2.8 fusion.61
  229.4 2.7 multiply_convert_fusion.2
  232.1 2.1 convolution_multiply_fusion.2
  237.2 2.4 copy.131
  239.6 9.0 %scatter_fusion = f32[32,128,128]{2,1,0:T(8,128)} fusion(f32[32,128,128]{2,1,0:T(8,128)} %get-tuple-element.190, s32[48]{0:T(128)S(1)} %reshape.166, f32[48,128,128]{2,1,0:T(8,128)S(1)} %copy.131), kind=kCustom, calls=%fused_computation.3.clone.1 | custom fusion | flops 786432 | bytes 9437376 | tf_op jit(solution)/shard_map/while/body/eval_jaxpr/scatter-add | solution.py:87
  248.6 2.8 fusion.61
  260.7 2.7 multiply_convert_fusion.2
  263.4 2.1 convolution_multiply_fusion.2
  268.5 2.4 copy.131
  270.8 9.1 %scatter_fusion = f32[32,128,128]{2,1,0:T(8,128)} fusion(f32[32,128,128]{2,1,0:T(8,128)} %get-tuple-element.190, s32[48]{0:T(128)S(1)} %reshape.166, f32[48,128,128]{2,1,0:T(8,128)S(1)} %copy.131), kind=kCustom, calls=%fused_computation.3.clone.1 | custom fusion | flops 786432 | bytes 9437376 | tf_op jit(solution)/shard_map/while/body/eval_jaxpr/scatter-add | solution.py:87
  279.9 2.8 fusion.61
  292.0 2.7 multiply_convert_fusion.2
  294.7 2.1 convolution_multiply_fusion.2
  297.8 2.0 pad_maximum_fusion.4
  299.8 2.4 copy.131
  302.2 9.1 %scatter_fusion = f32[32,128,128]{2,1,0:T(8,128)} fusion(f32[32,128,128]{2,1,0:T(8,128)} %get-tuple-element.190, s32[48]{0:T(128)S(1)} %reshape.166, f32[48,128,128]{2,1,0:T(8,128)S(1)} %copy.131), kind=kCustom, calls=%fused_computation.3.clone.1 | custom fusion | flops 786432 | bytes 9437376 | tf_op jit(solution)/shard_map/while/body/eval_jaxpr/scatter-add | solution.py:87
  311.2 2.8 fusion.61
  323.2 2.7 multiply_convert_fusion.2
  325.9 2.1 convolution_multiply_fusion.2
  329.0 2.0 pad_maximum_fusion.4
  331.0 2.4 copy.131
  333.4 9.1 %scatter_fusion = f32[32,128,128]{2,1,0:T(8,128)} fusion(f32[32,128,128]{2,1,0:T(8,128)} %get-tuple-element.190, s32[48]{0:T(128)S(1)} %reshape.166, f32[48,128,128]{2,1,0:T(8,128)S(1)} %copy.131), kind=kCustom, calls=%fused_computation.3.clone.1 | custom fusion | flops 786432 | bytes 9437376 | tf_op jit(solution)/shard_map/while/body/eval_jaxpr/scatter-add | solution.py:87
  342.5 2.8 fusion.61
  354.5 2.7 multiply_convert_fusion.2
  357.2 2.1 convolution_multiply_fusion.2
  360.2 2.0 pad_maximum_fusion.4
  362.3 2.4 copy.131
  364.6 9.1 %scatter_fusion = f32[32,128,128]{2,1,0:T(8,128)} fusion(f32[32,128,128]{2,1,0:T(8,128)} %get-tuple-element.190, s32[48]{0:T(128)S(1)} %reshape.166, f32[48,128,128]{2,1,0:T(8,128)S(1)} %copy.131), kind=kCustom, calls=%fused_computation.3.clone.1 | custom fusion | flops 786432 | bytes 9437376 | tf_op jit(solution)/shard_map/while/body/eval_jaxpr/scatter-add | solution.py:87
  373.7 2.8 fusion.61
  380.7 17.0 %gather_fusion.2 = bf16[4096,192]{1,0:T(8,128)(2,1)} fusion(bf16[4096,192]{1,0:T(8,128)(2,1)S(1)} %pad_maximum_fusion.2, s32[4096]{0:T(1024)S(1)} %broadcast_clamp_fusion), kind=kCustom, calls=%fused_computation.2 | custom fusion | bytes 3162112 | tf_op jit(solution)/shard_map/jit(_take)/gather | solution.py:97
  402.6 2.1 collective-permute-start.2
  405.8 3.1 collective-permute-start.4
  411.8 4.6 collective-permute-done.1
  419.4 11.1 %collective-permute-done.3 = bf16[512,1,192]{0,2,1:T(8,128)(2,1)} collective-permute-done((bf16[512,1,192]{0,2,1:T(8,128)(2,1)S(1)}, bf16[512,1,192]{0,2,1:T(8,128)(2,1)}, u32[]{:S(2)}, u32[]{:S(2)}) %collective-permute-start.3) | collective-permute-done | bytes 196640 | tf_op jit(solution)/shard_map/ppermute | solution.py:111
  431.4 4.1 collective-permute-done.4
  435.6 2.0 fusion.23
  438.9 2.1 bitcast_add_fusion
  441.0 14.5 %reduce-scatter.2.cloned.1.call-done = f32[256,1024]{1,0:T(8,128)} async-done(((f32[512,1024]{1,0:T(8,128)}), f32[256,1024]{1,0:T(8,128)}) %reduce-scatter.2.cloned.1.call-update) | async-done | bytes 1048592 | tf_op jit(solution)/shard_map/reduce_scatter | solution.py:125
  455.5 2.1 convert_element_type.17
  (229 shorter events, 106.7 us)
Async XLA Ops:
  6.5 14.1 %copy-start = (bf16[512,1024]{1,0:T(8,128)(2,1)S(1)}, bf16[512,1024]{1,0:T(8,128)(2,1)}, u32[]{:S(2)}) copy-start(bf16[512,1024]{1,0:T(8,128)(2,1)} %param.17) | copy-start | bytes 3145732
  6.5 3.2 copy-start.10
  6.5 14.1 %all-gather.2.cloned.1.call-start = ((), (), s32[]{:S(2)}) async-start(), calls=%async_computation.2 | async-start | bytes 1572864 | tf_op jit(solution)/shard_map/all_gather | solution.py:23
  24.5 6.1 %copy-start.12 = (s32[1,32,12]{1,0,2:T(1,128)S(1)}, s32[1,32,12]{1,0,2:T(1,128)}, u32[]{:S(2)}) copy-start(s32[1,32,12]{1,0,2:T(1,128)} %param.22) | copy-start | bytes 4612
  24.5 6.2 %copy-start.6 = (bf16[1024,512]{1,0:T(8,128)(2,1)S(1)}, bf16[1024,512]{1,0:T(8,128)(2,1)}, u32[]{:S(2)}) copy-start(bf16[1024,512]{1,0:T(8,128)(2,1)} %param.18) | copy-start | bytes 3145732
  24.5 54.6 %all-to-all-start = ((bf16[512,8,256]{0,2,1:T(8,128)(2,1)}), bf16[512,8,256]{0,2,1:T(8,128)(2,1)S(1)}, u32[]{:S(2)}, u32[]{:S(2)}) async-start(bf16[512,8,256]{0,2,1:T(8,128)(2,1)} %bitcast.137), calls=%async_computation | async-start | bytes 4194304 | tf_op jit(solution)/shard_map/all_to_all | solution.py:33
  30.4 425.1 %reduce-scatter.2.cloned.1.call-start = ((), (), s32[]{:S(2)}) async-start(), calls=%async_computation.3 | async-start | bytes 3145728 | tf_op jit(solution)/shard_map/reduce_scatter | solution.py:125
  32.0 2.4 copy-start.7
  32.0 3.7 copy-start.11
  32.0 19.5 %copy-start.13 = (s32[1,32]{1,0:T(1,128)S(1)}, s32[1,32]{1,0:T(1,128)}, u32[]{:S(2)}) copy-start(s32[1,32]{1,0:T(1,128)} %param.23) | copy-start | bytes 388
  79.1 1.3 copy-start.5
  126.2 2.9 copy-start.3
  131.1 4.3 copy-start.2
  154.7 2.8 copy-start.4
  157.5 2.9 copy-start.3
  162.4 4.3 copy-start.2
  186.0 2.8 copy-start.4
  188.9 2.9 copy-start.3
  193.8 4.3 copy-start.2
  217.4 2.8 copy-start.4
  220.2 2.9 copy-start.3
  225.1 4.3 copy-start.2
  248.6 2.8 copy-start.4
  251.4 2.9 copy-start.3
  256.3 4.3 copy-start.2
  279.9 2.8 copy-start.4
  282.7 2.9 copy-start.3
  287.7 4.3 copy-start.2
  311.2 2.8 copy-start.4
  314.0 2.9 copy-start.3
  319.0 4.2 copy-start.2
  342.5 2.8 copy-start.4
  345.3 2.9 copy-start.3
  350.2 4.2 copy-start.2
  373.7 2.8 copy-start.4
  400.8 8.5 %collective-permute-start = (bf16[512,1,192]{0,2,1:T(8,128)(2,1)}, bf16[512,1,192]{0,2,1:T(8,128)(2,1)}, u32[]{:S(2)}, u32[]{:S(2)}) collective-permute-start(bf16[512,1,192]{0,2,1:T(8,128)(2,1)} %bitcast.33), channel_id=1, source_target_pairs={{0,2},{2,0},{4,6},{6,4},{8,10},{10,8},{12,14},{14,12},{1,3},{3,1},... | collective-permute-start | bytes 589832 | tf_op jit(solution)/shard_map/ppermute | solution.py:111
  402.4 14.0 %collective-permute-start.1 = (bf16[512,1,192]{0,2,1:T(8,128)(2,1)S(1)}, bf16[512,1,192]{0,2,1:T(8,128)(2,1)}, u32[]{:S(2)}, u32[]{:S(2)}) collective-permute-start(bf16[512,1,192]{0,2,1:T(8,128)(2,1)S(1)} %bitcast.156), channel_id=1, source_target_pairs={{0,4},{2,6},{4,0},{6,2},{8,12},{10,14},{12,8},{14,10},{1,5},{3,7},... | collective-permute-start | bytes 589832 | tf_op jit(solution)/shard_map/ppermute | solution.py:111
  402.6 15.9 %collective-permute-start.2 = (bf16[512,1,192]{0,2,1:T(8,128)(2,1)S(1)}, bf16[512,1,192]{0,2,1:T(8,128)(2,1)}, u32[]{:S(2)}, u32[]{:S(2)}) collective-permute-start(bf16[512,1,192]{0,2,1:T(8,128)(2,1)S(1)} %bitcast.154), channel_id=1, source_target_pairs={{0,6},{2,4},{4,2},{6,0},{8,14},{10,12},{12,10},{14,8},{1,7},{3,5},... | collective-permute-start | bytes 589832 | tf_op jit(solution)/shard_map/ppermute | solution.py:111
  404.8 25.7 %collective-permute-start.3 = (bf16[512,1,192]{0,2,1:T(8,128)(2,1)S(1)}, bf16[512,1,192]{0,2,1:T(8,128)(2,1)}, u32[]{:S(2)}, u32[]{:S(2)}) collective-permute-start(bf16[512,1,192]{0,2,1:T(8,128)(2,1)S(1)} %bitcast.153), channel_id=1, source_target_pairs={{0,8},{2,10},{4,12},{6,14},{8,0},{10,2},{12,4},{14,6},{1,9},{3,11}... | collective-permute-start | bytes 589832 | tf_op jit(solution)/shard_map/ppermute | solution.py:111
  405.8 29.7 %collective-permute-start.4 = (bf16[512,1,192]{0,2,1:T(8,128)(2,1)S(1)}, bf16[512,1,192]{0,2,1:T(8,128)(2,1)S(1)}, u32[]{:S(2)}, u32[]{:S(2)}) collective-permute-start(bf16[512,1,192]{0,2,1:T(8,128)(2,1)S(1)} %bitcast.152), channel_id=1, source_target_pairs={{0,10},{2,8},{4,14},{6,12},{8,2},{10,0},{12,6},{14,4},{1,11},{3,9}... | collective-permute-start | bytes 589832 | tf_op jit(solution)/shard_map/ppermute | solution.py:111
  409.3 26.2 %collective-permute-start.5 = (bf16[512,1,192]{0,2,1:T(8,128)(2,1)S(1)}, bf16[512,1,192]{0,2,1:T(8,128)(2,1)S(1)}, u32[]{:S(2)}, u32[]{:S(2)}) collective-permute-start(bf16[512,1,192]{0,2,1:T(8,128)(2,1)S(1)} %bitcast.155), channel_id=1, source_target_pairs={{0,12},{2,14},{4,8},{6,10},{8,4},{10,6},{12,0},{14,2},{1,13},{3,15... | collective-permute-start | bytes 589832 | tf_op jit(solution)/shard_map/ppermute | solution.py:111
  416.4 19.2 %collective-permute-start.6 = (bf16[512,1,192]{0,2,1:T(8,128)(2,1)S(1)}, bf16[512,1,192]{0,2,1:T(8,128)(2,1)S(1)}, u32[]{:S(2)}, u32[]{:S(2)}) collective-permute-start(bf16[512,1,192]{0,2,1:T(8,128)(2,1)S(1)} %bitcast.151), channel_id=1, source_target_pairs={{0,14},{2,12},{4,10},{6,8},{8,6},{10,4},{12,2},{14,0},{1,15},{3,13... | collective-permute-start | bytes 589832 | tf_op jit(solution)/shard_map/ppermute | solution.py:111
  435.6 2.1 copy-start.9
  437.7 1.2 copy-start.8
  438.9 18.7 %copy-start.1 = (bf16[512,1024]{1,0:T(8,128)(2,1)S(1)}, bf16[512,1024]{1,0:T(8,128)(2,1)}, u32[]{:S(2)}) copy-start(bf16[512,1024]{1,0:T(8,128)(2,1)} %param.17) | copy-start | bytes 3145732
Sparse Core Ops, SparseCore 0:
  8.9 11.7 all-gather.1
  441.1 14.2 reduce-scatter.1
